TPU v7x, 256 devices: a whole 4x4x8 slice. The times are simulated.
256 devices in a mesh: grp: 8 (over x, core), vocab: 32 (over y, z).
Axes of the slice: x: 4, y: 4, z: 8, core: 2. Of those that a mesh axis runs over, the one named last changes fastest.
Arguments:
- hidden: bfloat16 [1024, 16384], P('grp', 'vocab'), may hold values from -6 to 6
- flags: int32 [1024, 1], P('grp'), may hold values from 0 to 8; in each aligned block of 128 rows (0 to 127, 128 to 255, ...) at most 16 rows name the same one
- targets: int32 [1024], P('grp'), may hold values from 0 to 65535
- head: bfloat16 [16384, 65536], P('grp', 'vocab'), may hold values from -0.140625 to 0.140625
- lengths: int32 [8, 8], P('grp'), may hold values from 1 to 64, 128 in all within a row
Outputs:
- token_scores: float32 [1024], P('grp')
- doc_scores: float32 [8, 8], P('grp')
Inputs may be any that keep to these rules, and one draw needn't show every extreme that they name: `flags`: A value below 8 names the scorer group of a scored row. Within the 128 rows of one shard no value occurs more than 16 times, and in every draw some value occurs exactly 16 times in some shard.
All inputs are finite; a program needn't handle non-finite values.
Results may differ from a plain program's by a relative error of at most 0.0003.
Values may be sent and summed in bfloat16 or wider, within the bound.
A program may use at most 128 MiB of HBM per device.

v0:
```python
import jax
import jax.numpy as jnp
from jax import lax
from jax.sharding import PartitionSpec as P


def combined_all(part, axis, combine):
    gathered = jax.tree.map(lambda a: lax.all_gather(a, axis), part)

    def take(source):
        return jax.tree.map(lambda a: lax.dynamic_index_in_dim(a, source, 0, False), gathered)

    return lax.fori_loop(
        1, lax.axis_size(axis), lambda source, state: combine(state, take(source)), take(0)
    )


def slot_table(flag_col, groups, capacity, shard_rows):
    values = jnp.arange(groups + 1, dtype=jnp.int32)
    onehot = (flag_col[:, None] == values[None, :]).astype(jnp.int32)
    ranking = jnp.sum((jnp.cumsum(onehot, axis=0) - 1) * onehot, axis=1)
    where_to = jnp.where(flag_col < groups, flag_col * capacity + ranking, groups * capacity)
    table = jnp.full((groups * capacity + 1,), -1, jnp.int32)
    table = table.at[where_to].set(jnp.arange(shard_rows, dtype=jnp.int32))
    return table[: groups * capacity]


def combine_stats(left, right):
    row_max = jnp.maximum(left[0], right[0])
    left_gap = left[0] - row_max
    right_gap = right[0] - row_max
    left_fac = jnp.exp(left_gap)
    right_fac = jnp.exp(right_gap)
    row_total = left_fac * left[1] + right_fac * right[1]
    first_mom = left_fac * (left[2] + left_gap * left[1]) + right_fac * (
        right[2] + right_gap * right[1]
    )
    second_mom = left_fac * (left[3] + 2.0 * left_gap * left[2] + left_gap * left_gap * left[1])
    second_mom = second_mom + right_fac * (
        right[3] + 2.0 * right_gap * right[2] + right_gap * right_gap * right[1]
    )
    return (row_max, row_total, first_mom, second_mom)


def local_stats(logits, target_ids, columns, axis):
    row_max = jnp.max(logits, axis=axis)
    shifted = logits - jnp.expand_dims(row_max, axis)
    scaled = jnp.exp(shifted)
    row_total = jnp.sum(scaled, axis=axis)
    first_mom = jnp.sum(scaled * shifted, axis=axis)
    second_mom = jnp.sum(scaled * shifted * shifted, axis=axis)
    is_target = target_ids[:, None] == columns[None, :]
    target_val = jnp.sum(jnp.where(is_target, logits, jnp.float32(0.0)), axis=axis)
    return (row_max, row_total, first_mom, second_mom, target_val)


def final_scores(target_ids, row_max, row_total, first_mom, second_mom, target_val):
    mean_shift = first_mom / row_total
    row_var = second_mom / row_total - mean_shift * mean_shift
    return jnp.where(
        target_ids >= 0,
        (target_val - row_max - mean_shift) / jnp.sqrt(jnp.maximum(row_var, 1.0)),
        jnp.float32(0.0),
    )


def shards(hidden, flags, targets, head, lengths):
    groups = lax.axis_size("grp")
    shard_rows = hidden.shape[0]
    capacity = shard_rows // groups
    vocab_dev = head.shape[1]
    my_vocab = lax.axis_index("vocab")
    flag_col = flags[:, 0]
    table = slot_table(flag_col, groups, capacity, shard_rows)
    is_live = table >= 0
    safe_rows = jnp.maximum(table, 0)
    pieces = jnp.where(is_live[:, None], hidden[safe_rows], jnp.zeros((), jnp.bfloat16))
    slot_targets = jnp.where(is_live, targets[safe_rows], -1)
    arrived = lax.all_to_all(
        pieces.reshape(groups, capacity, pieces.shape[1]),
        "grp",
        split_axis=0,
        concat_axis=0,
        tiled=True,
    )
    full_rows = lax.all_gather(
        arrived.reshape(shard_rows, pieces.shape[1]), "vocab", axis=1, tiled=True
    )
    block_rows = lax.all_to_all(full_rows, "grp", split_axis=1, concat_axis=0, tiled=True)
    target_ids = lax.all_to_all(
        slot_targets.reshape(groups, capacity), "grp", split_axis=0, concat_axis=0, tiled=True
    ).reshape(shard_rows)
    logits = lax.psum_scatter(
        jnp.dot(block_rows, head, preferred_element_type=jnp.float32),
        "grp",
        scatter_dimension=0,
        tiled=True,
    )
    columns = my_vocab * vocab_dev + jnp.arange(vocab_dev, dtype=jnp.int32)
    row_max, row_total, first_mom, second_mom, target_val = local_stats(
        logits, target_ids, columns, 1
    )
    row_max, row_total, first_mom, second_mom = combined_all(
        (row_max, row_total, first_mom, second_mom), "vocab", combine_stats
    )
    target_val = lax.psum(target_val, "vocab")
    token_scores = final_scores(target_ids, row_max, row_total, first_mom, second_mom, target_val)
    returned = lax.all_to_all(
        token_scores.reshape(groups, capacity), "grp", split_axis=0, concat_axis=0, tiled=True
    ).reshape(shard_rows)
    row_val = (
        jnp.zeros((shard_rows + 1,), jnp.float32)
        .at[jnp.where(is_live, table, shard_rows)]
        .set(returned)[:shard_rows]
    )
    flagged = (flag_col < groups).astype(jnp.float32)
    doc_ends = jnp.cumsum(lengths[0])
    doc_starts = doc_ends - lengths[0]
    positions = jnp.arange(shard_rows, dtype=jnp.int32)
    membership = (
        (positions[None, :] >= doc_starts[:, None]) & (positions[None, :] < doc_ends[:, None])
    ).astype(jnp.float32)
    sums = jnp.sum(membership * row_val[None, :], axis=1)
    counts = jnp.sum(membership * flagged[None, :], axis=1)
    doc_means = (sums / jnp.maximum(counts, 1.0))[None, :]
    return (token_scores, doc_means)


def solution(mesh):
    placed = (P("grp", "vocab"), P("grp", None), P("grp"), P("grp", "vocab"), P("grp", None))
    return jax.shard_map(
        shards, mesh=mesh, in_specs=placed, out_specs=(P("grp"), P("grp", None)), check_vma=False
    )
```

profile of v0, /device:TPU:1, one launch (start us, length us, event | category | flops | bytes accessed | tf_op | source)
XLA Modules:
  0.0 488.9 jit_solution(7191298796290074408)
XLA Ops:
  7.2 0.8 fusion.12
  8.2 0.8 select_reduce_fusion.1
  9.0 0.7 fusion.19
  9.7 1.0 scatter_custom_fusion
  10.8 0.9 gather_fusion.1
  11.7 11.6 %all_to_all.39 = bf16[8,16,512]{2,1,0:T(8,128)(2,1)} all-to-all(bf16[8,16,512]{2,1,0:T(8,128)(2,1)S(1)} %broadcast_select_fusion), channel_id=1, replica_groups=mesh['grp'=8,'vocab'=32] {'grp'}, dimensions={0} | all-to-all | bytes 262144 | tf_op jit(solution)/shard_map/all_to_all | solution.py:79
  23.4 80.8 %all-gather.10.cloned.1.call-done = bf16[128,16384]{1,0:T(8,128)(2,1)} async-done(((bf16[128,512]{1,0:T(8,128)(2,1)}), bf16[128,16384]{1,0:T(8,128)(2,1)}) %all-gather.10.cloned.1.call-update) | async-done | bytes 4194320 | tf_op jit(solution)/shard_map/all_gather | solution.py:86
  104.2 6.4 %copy.16 = bf16[128,16384]{0,1:T(8,128)(2,1)} copy(bf16[128,16384]{1,0:T(8,128)(2,1)} %all-gather.10.cloned.1.call-done) | data formatting | bytes 8388608 | tf_op jit(solution)/shard_map/all_gather | solution.py:86
  110.6 57.6 %all_to_all.40 = bf16[128,8,2048]{0,2,1:T(8,128)(2,1)} all-to-all(bf16[128,8,2048]{0,2,1:T(8,128)(2,1)} %bitcast.91), channel_id=1, replica_groups=mesh['grp'=8,'vocab'=32] {'grp'}, dimensions={1} | all-to-all | bytes 8388608 | tf_op jit(solution)/shard_map/all_to_all | solution.py:89
  168.2 6.5 %copy.17 = bf16[8,128,2048]{2,1,0:T(8,128)(2,1)} copy(bf16[8,128,2048]{1,2,0:T(8,128)(2,1)} %bitcast.92) | data formatting | bytes 8388608 | tf_op jit(solution)/shard_map/all_to_all | solution.py:89
  174.6 14.4 %fusion.21 = f32[1024,2048]{1,0:T(8,128)} fusion(bf16[1024,2048]{1,0:T(8,128)(2,1)} %bitcast.93, bf16[2048,2048]{1,0:T(8,128)(2,1)} %param.10), kind=kOutput, calls=%fused_computation.58 | convolution fusion | flops 8589934592 | bytes 20971520 | tf_op jit(solution)/shard_map/dot_general | solution.py:94
  189.1 0.6 copy-done.1
  189.7 1.2 gather_fusion
  191.0 0.7 select_n.65
  191.6 4.2 all-to-all-start
  196.1 4.4 all-to-all-done
  201.0 0.7 reduce.6
  201.7 40.7 %reduce-scatter.2.cloned.1.call-done = f32[128,2048]{1,0:T(8,128)} async-done(((f32[1024,2048]{1,0:T(8,128)}), f32[128,2048]{1,0:T(8,128)}) %reduce-scatter.2.cloned.1.call-update) | async-done | bytes 1048592 | tf_op jit(solution)/shard_map/reduce_scatter | solution.py:93
  242.4 1.4 reduce_max.9
  243.8 31.7 %all-gather.4 = f32[32,1,128]{2,1,0:T(1,128)S(1)} all-gather(f32[1,1,128]{2,1,0:T(1,128)S(1)} %bitcast.100), channel_id=2, replica_groups=mesh['grp'=8,'vocab'=32] {'vocab'}, dimensions={0}, use_global_device_ids=true | all-gather | bytes 16896 | tf_op jit(solution)/shard_map/all_gather | solution.py:8
  275.4 1.7 fusion.11
  277.2 27.1 %all-gather.5 = f32[32,1,128]{2,1,0:T(1,128)S(1)} all-gather(f32[1,1,128]{2,1,0:T(1,128)S(1)} %bitcast.103), channel_id=3, replica_groups=mesh['grp'=8,'vocab'=32] {'vocab'}, dimensions={0}, use_global_device_ids=true | all-gather | bytes 16896 | tf_op jit(solution)/shard_map/all_gather | solution.py:8
  304.3 28.7 %all-gather.6 = f32[32,1,128]{2,1,0:T(1,128)S(1)} all-gather(f32[1,1,128]{2,1,0:T(1,128)S(1)} %bitcast.102), channel_id=4, replica_groups=mesh['grp'=8,'vocab'=32] {'vocab'}, dimensions={0}, use_global_device_ids=true | all-gather | bytes 16896 | tf_op jit(solution)/shard_map/all_gather | solution.py:8
  333.0 27.2 %all-gather.7 = f32[32,1,128]{2,1,0:T(1,128)S(1)} all-gather(f32[1,1,128]{2,1,0:T(1,128)S(1)} %bitcast.101), channel_id=5, replica_groups=mesh['grp'=8,'vocab'=32] {'vocab'}, dimensions={0}, use_global_device_ids=true | all-gather | bytes 16896 | tf_op jit(solution)/shard_map/all_gather | solution.py:8
  360.2 2.7 while.21
  362.9 56.7 %psum.7 = f32[128]{0:T(128)S(1)} all-reduce(f32[128]{0:T(128)S(1)} %get-tuple-element.232), channel_id=1, replica_groups=mesh['grp'=8,'vocab'=32] {'vocab'}, use_global_device_ids=true, to_apply=%region_5.6 | all-reduce | flops 128 | bytes 1024 | tf_op jit(solution)/shard_map/psum | solution.py:106
  419.6 0.7 all_to_all.33
  420.3 54.2 %all-to-all-start.3 = ((f32[8,1,16]{2,1,0:T(1,128)}), f32[8,1,16]{2,1,0:T(1,128)S(1)}, u32[]{:S(2)}, u32[]{:S(2)}) async-start(f32[8,1,16]{2,1,0:T(1,128)} %bitcast.28), calls=%async_computation.4 | async-start | bytes 8192 | tf_op jit(solution)/shard_map/all_to_all | solution.py:108
  474.5 4.6 all-to-all-done.3
  479.6 0.7 reduce.7
  480.3 1.0 scatter_custom_fusion.1
  481.5 0.5 fusion.18
  (129 shorter events, 3.9 us)
Async XLA Ops:
  7.2 3.6 copy-start
  7.2 97.0 %all-gather.10.cloned.1.call-start = ((), (), s32[]{:S(2)}) async-start(), calls=%async_computation.5 | async-start | bytes 4325376 | tf_op jit(solution)/shard_map/all_gather | solution.py:86
  23.3 219.1 %reduce-scatter.2.cloned.1.call-start = ((), (), s32[]{:S(2)}) async-start(), calls=%async_computation.6 | async-start | bytes 9437184 | tf_op jit(solution)/shard_map/reduce_scatter | solution.py:93
  189.1 0.7 copy-start.1
  189.1 6.8 %copy-start.4 = (s32[1,8]{1,0:T(1,128)S(1)}, s32[1,8]{1,0:T(1,128)}, u32[]{:S(2)}) copy-start(s32[1,8]{1,0:T(1,128)} %param.11) | copy-start | bytes 100
  189.1 285.4 %copy-start.2 = (s32[128,1]{0,1:T(1,128)S(1)}, s32[128,1]{0,1:T(1,128)}, u32[]{:S(2)}) copy-start(s32[128,1]{0,1:T(1,128)} %param.8) | copy-start | bytes 1540
  191.6 8.8 %all-to-all-start = ((s32[8,1,16]{2,1,0:T(1,128)}), s32[8,1,16]{2,1,0:T(1,128)S(1)}, u32[]{:S(2)}, u32[]{:S(2)}) async-start(s32[8,1,16]{2,1,0:T(1,128)} %bitcast.7), calls=%async_computation | async-start | bytes 8192 | tf_op jit(solution)/shard_map/all_to_all | solution.py:90
  419.6 62.5 %copy-start.3 = (f32[128]{0:T(128)}, f32[128]{0:T(128)S(1)}, u32[]{:S(2)}) copy-start(f32[128]{0:T(128)S(1)} %compare_select_fusion.2) | copy-start | bytes 1540
  420.3 58.8 %all-to-all-start.3 = ((f32[8,1,16]{2,1,0:T(1,128)}), f32[8,1,16]{2,1,0:T(1,128)S(1)}, u32[]{:S(2)}, u32[]{:S(2)}) async-start(f32[8,1,16]{2,1,0:T(1,128)} %bitcast.28), calls=%async_computation.4 | async-start | bytes 8192 | tf_op jit(solution)/shard_map/all_to_all | solution.py:108
Sparse Core Ops, SparseCore 0:
  23.4 80.6 all-gather.9
  189.2 53.1 reduce-scatter.1
where the time goes:
time: 490 us; the launch traced here: 489 us
  blocking collectives  241 us (49%)
  waiting for transfers between devices  131 us (27%)
  starting transfers between devices  58.5 us (12%)
  local copies, waits for them, and re-layouts  20.2 us (4%)
  matrix products  14.4 us (3%)
  between operations  14.2 us (3%)
  other arithmetic  9.6 us (2%)
    all_gather x4, blocking collectives, combined_all(): gathered = jax.tree.map(lambda a: lax.all_gather(a, axis), part)  115 us
    all_gather x1, waiting for transfers between devices, shards(): lax.all_gather(arrived.reshape(shard_rows, pieces.shape[1]), 'vocab', axi...  80.8 us
    all_to_all x1, blocking collectives, shards(): lax.all_to_all(full_rows, 'grp', split_axis=1, concat_axis=0, tiled=True)  57.6 us
    psum x1, blocking collectives, shards(): target_val = lax.psum(target_val, 'vocab')  56.7 us
    all_to_all x1, starting transfers between devices, shards(): lax.all_to_all(token_scores.reshape(groups, capacity), 'grp', split_axis=...  54.2 us
    reduce_scatter x1, waiting for transfers between devices, shards(): lax.psum_scatter(jnp.dot(block_rows, head, preferred_element_type=jnp.flo...  40.7 us
    dot_general x1, matrix products, shards(): jnp.dot(block_rows, head, preferred_element_type=jnp.float32)  14.4 us
    all_to_all x1, blocking collectives, shards(): lax.all_to_all(pieces.reshape(groups, capacity, pieces.shape[1]), 'grp',...  11.6 us
  transfers between devices with their start and end apart: 4, of which 4 were waited for; matrix products, arithmetic and copies ran while one was open for 1% of the time, Pallas kernels for 0%

commit v1 on v0

--- a/solution.py
+++ b/solution.py
@@ -2,6 +2,11 @@
 import jax.numpy as jnp
 from jax import lax
 from jax.sharding import PartitionSpec as P
+
+
+def gather_by_exchange(x, axis, dim):
+    copies = jnp.concatenate([x] * lax.axis_size(axis), axis=dim)
+    return lax.all_to_all(copies, axis, dim, dim, tiled=True)
 
 
 def combined_all(part, axis, combine):
@@ -83,9 +88,7 @@
         concat_axis=0,
         tiled=True,
     )
-    full_rows = lax.all_gather(
-        arrived.reshape(shard_rows, pieces.shape[1]), "vocab", axis=1, tiled=True
-    )
+    full_rows = gather_by_exchange(arrived.reshape(shard_rows, pieces.shape[1]), "vocab", 1)
     block_rows = lax.all_to_all(full_rows, "grp", split_axis=1, concat_axis=0, tiled=True)
     target_ids = lax.all_to_all(
         slot_targets.reshape(groups, capacity), "grp", split_axis=0, concat_axis=0, tiled=True

time: 490 us -> 502 us (1.024)
  blocking collectives: 241 us -> 343 us
  waiting for transfers between devices: 131 us -> 45.9 us
  local copies, waits for them, and re-layouts: 20.2 us -> 14.9 us
    all_to_all x0 -> x1, blocking collectives: none -> 103 us  [gather_by_exchange(): return lax.all_to_all(copies, axis, dim, dim, tiled=True)]
    all_gather x1 -> x0, waiting for transfers between devices: 80.8 us -> none  [shards(): lax.all_gather(arrived.reshape(shard_rows, pieces.shape[1]), 'vocab', axi...]
    all_gather x1 -> x0, local copies, waits for them, and re-layouts: 6.37 us -> none  [shards(): lax.all_gather(arrived.reshape(shard_rows, pieces.shape[1]), 'vocab', axi...]
  transfers between devices with their start and end apart: 4 -> 3, of which waited for: 4 -> 3; matrix products, arithmetic and copies ran while one was open for 1% -> 1% of each run, Pallas kernels for 0% -> 0%
where the time goes in v1:
time: 502 us; the launch traced here: 501 us
  blocking collectives  343 us (68%)
  starting transfers between devices  58.5 us (12%)
  waiting for transfers between devices  45.9 us (9%)
  local copies, waits for them, and re-layouts  14.9 us (3%)
  matrix products  14.4 us (3%)
  between operations  14.2 us (3%)
  other arithmetic  9.59 us (2%)
    all_gather x4, blocking collectives, combined_all(): gathered = jax.tree.map(lambda a: lax.all_gather(a, axis), part)  115 us
    all_to_all x1, blocking collectives, gather_by_exchange(): return lax.all_to_all(copies, axis, dim, dim, tiled=True)  103 us
    all_to_all x1, blocking collectives, shards(): lax.all_to_all(full_rows, 'grp', split_axis=1, concat_axis=0, tiled=True)  57.5 us
    psum x1, blocking collectives, shards(): target_val = lax.psum(target_val, 'vocab')  56.7 us
    all_to_all x1, starting transfers between devices, shards(): lax.all_to_all(token_scores.reshape(groups, capacity), 'grp', split_axis=...  54.2 us
    reduce_scatter x1, waiting for transfers between devices, shards(): lax.psum_scatter(jnp.dot(block_rows, head, preferred_element_type=jnp.flo...  36.9 us
    dot_general x1, matrix products, shards(): jnp.dot(block_rows, head, preferred_element_type=jnp.float32)  14.4 us
    all_to_all x1, blocking collectives, shards(): lax.all_to_all(pieces.reshape(groups, capacity, pieces.shape[1]), 'grp',...  10.9 us
  transfers between devices with their start and end apart: 3, of which 3 were waited for; matrix products, arithmetic and copies ran while one was open for 1% of the time, Pallas kernels for 0%

profile of v1, /device:TPU:1, one launch (start us, length us, event | category | flops | bytes accessed | tf_op | source)
XLA Modules:
  0.0 501.2 jit_solution(1470044901767615267)
XLA Ops:
  7.2 0.8 fusion.12
  8.2 0.8 select_reduce_fusion.1
  9.0 0.7 fusion.19
  9.7 1.0 scatter_custom_fusion
  10.8 0.9 gather_fusion.1
  11.7 10.9 %all_to_all.45 = bf16[8,16,512]{2,1,0:T(8,128)(2,1)S(1)} all-to-all(bf16[8,16,512]{2,1,0:T(8,128)(2,1)S(1)} %broadcast_select_fusion), channel_id=1, replica_groups=mesh['grp'=8,'vocab'=32] {'grp'}, dimensions={0} | all-to-all | bytes 262144 | tf_op jit(solution)/shard_map/all_to_all | solution.py:84
  22.7 0.9 concatenate.7
  23.7 103.1 %all_to_all.46 = bf16[128,32,512]{0,2,1:T(8,128)(2,1)S(1)} all-to-all(bf16[128,32,512]{0,2,1:T(8,128)(2,1)S(1)} %concatenate.7), channel_id=1, replica_groups=mesh['grp'=8,'vocab'=32] {'vocab'}, dimensions={1} | all-to-all | bytes 8388608 | tf_op jit(solution)/shard_map/all_to_all | solution.py:9
  126.8 57.5 %all_to_all.47 = bf16[128,8,2048]{0,2,1:T(8,128)(2,1)} all-to-all(bf16[128,8,2048]{0,2,1:T(8,128)(2,1)S(1)} %bitcast.91), channel_id=1, replica_groups=mesh['grp'=8,'vocab'=32] {'grp'}, dimensions={1} | all-to-all | bytes 8388608 | tf_op jit(solution)/shard_map/all_to_all | solution.py:92
  184.3 6.5 %copy.15 = bf16[8,128,2048]{2,1,0:T(8,128)(2,1)} copy(bf16[8,128,2048]{1,2,0:T(8,128)(2,1)} %bitcast.92) | data formatting | bytes 8388608 | tf_op jit(solution)/shard_map/all_to_all | solution.py:92
  190.8 14.4 %fusion.21 = f32[1024,2048]{1,0:T(8,128)} fusion(bf16[1024,2048]{1,0:T(8,128)(2,1)} %bitcast.93, bf16[2048,2048]{1,0:T(8,128)(2,1)} %param.10), kind=kOutput, calls=%fused_computation.58 | convolution fusion | flops 8589934592 | bytes 20971520 | tf_op jit(solution)/shard_map/dot_general | solution.py:97
  205.2 0.6 copy-done.1
  205.8 1.2 gather_fusion
  207.1 0.7 select_n.65
  207.8 4.3 all-to-all-start
  212.2 4.4 all-to-all-done
  217.1 0.7 reduce.6
  217.9 36.9 %reduce-scatter.2.cloned.1.call-done = f32[128,2048]{1,0:T(8,128)} async-done(((f32[1024,2048]{1,0:T(8,128)}), f32[128,2048]{1,0:T(8,128)}) %reduce-scatter.2.cloned.1.call-update) | async-done | bytes 1048592 | tf_op jit(solution)/shard_map/reduce_scatter | solution.py:96
  254.7 1.4 reduce_max.9
  256.1 31.6 %all-gather.4 = f32[32,1,128]{2,1,0:T(1,128)S(1)} all-gather(f32[1,1,128]{2,1,0:T(1,128)S(1)} %bitcast.100), channel_id=2, replica_groups=mesh['grp'=8,'vocab'=32] {'vocab'}, dimensions={0}, use_global_device_ids=true | all-gather | bytes 16896 | tf_op jit(solution)/shard_map/all_gather | solution.py:13
  287.7 1.7 fusion.11
  289.5 27.1 %all-gather.5 = f32[32,1,128]{2,1,0:T(1,128)S(1)} all-gather(f32[1,1,128]{2,1,0:T(1,128)S(1)} %bitcast.103), channel_id=3, replica_groups=mesh['grp'=8,'vocab'=32] {'vocab'}, dimensions={0}, use_global_device_ids=true | all-gather | bytes 16896 | tf_op jit(solution)/shard_map/all_gather | solution.py:13
  316.6 28.8 %all-gather.6 = f32[32,1,128]{2,1,0:T(1,128)S(1)} all-gather(f32[1,1,128]{2,1,0:T(1,128)S(1)} %bitcast.102), channel_id=4, replica_groups=mesh['grp'=8,'vocab'=32] {'vocab'}, dimensions={0}, use_global_device_ids=true | all-gather | bytes 16896 | tf_op jit(solution)/shard_map/all_gather | solution.py:13
  345.3 27.2 %all-gather.7 = f32[32,1,128]{2,1,0:T(1,128)S(1)} all-gather(f32[1,1,128]{2,1,0:T(1,128)S(1)} %bitcast.101), channel_id=5, replica_groups=mesh['grp'=8,'vocab'=32] {'vocab'}, dimensions={0}, use_global_device_ids=true | all-gather | bytes 16896 | tf_op jit(solution)/shard_map/all_gather | solution.py:13
  372.5 2.7 while.21
  375.2 56.7 %psum.7 = f32[128]{0:T(128)S(1)} all-reduce(f32[128]{0:T(128)S(1)} %get-tuple-element.232), channel_id=1, replica_groups=mesh['grp'=8,'vocab'=32] {'vocab'}, use_global_device_ids=true, to_apply=%region_5.6 | all-reduce | flops 128 | bytes 1024 | tf_op jit(solution)/shard_map/psum | solution.py:109
  431.9 0.7 all_to_all.38
  432.6 54.2 %all-to-all-start.4 = ((f32[8,1,16]{2,1,0:T(1,128)}), f32[8,1,16]{2,1,0:T(1,128)S(1)}, u32[]{:S(2)}, u32[]{:S(2)}) async-start(f32[8,1,16]{2,1,0:T(1,128)} %bitcast.28), calls=%async_computation.5 | async-start | bytes 8192 | tf_op jit(solution)/shard_map/all_to_all | solution.py:111
  486.8 4.6 all-to-all-done.4
  491.9 0.7 reduce.7
  492.7 1.0 scatter_custom_fusion.1
  493.9 0.5 fusion.18
  (128 shorter events, 3.9 us)
Async XLA Ops:
  7.2 3.6 copy-start
  7.2 247.6 %reduce-scatter.2.cloned.1.call-start = ((), (), s32[]{:S(2)}) async-start(), calls=%async_computation.6 | async-start | bytes 9437184 | tf_op jit(solution)/shard_map/reduce_scatter | solution.py:96
  205.2 0.7 copy-start.1
  205.2 6.8 %copy-start.4 = (s32[1,8]{1,0:T(1,128)S(1)}, s32[1,8]{1,0:T(1,128)}, u32[]{:S(2)}) copy-start(s32[1,8]{1,0:T(1,128)} %param.11) | copy-start | bytes 100
  205.2 281.6 %copy-start.2 = (s32[128,1]{0,1:T(1,128)S(1)}, s32[128,1]{0,1:T(1,128)}, u32[]{:S(2)}) copy-start(s32[128,1]{0,1:T(1,128)} %param.8) | copy-start | bytes 1540
  207.8 8.8 %all-to-all-start = ((s32[8,1,16]{2,1,0:T(1,128)}), s32[8,1,16]{2,1,0:T(1,128)S(1)}, u32[]{:S(2)}, u32[]{:S(2)}) async-start(s32[8,1,16]{2,1,0:T(1,128)} %bitcast.7), calls=%async_computation | async-start | bytes 8192 | tf_op jit(solution)/shard_map/all_to_all | solution.py:93
  431.9 62.5 %copy-start.3 = (f32[128]{0:T(128)}, f32[128]{0:T(128)S(1)}, u32[]{:S(2)}) copy-start(f32[128]{0:T(128)S(1)} %compare_select_fusion.2) | copy-start | bytes 1540
  432.6 58.8 %all-to-all-start.4 = ((f32[8,1,16]{2,1,0:T(1,128)}), f32[8,1,16]{2,1,0:T(1,128)S(1)}, u32[]{:S(2)}, u32[]{:S(2)}) async-start(f32[8,1,16]{2,1,0:T(1,128)} %bitcast.28), calls=%async_computation.5 | async-start | bytes 8192 | tf_op jit(solution)/shard_map/all_to_all | solution.py:111
Sparse Core Ops, SparseCore 0:
  205.3 49.3 reduce-scatter.1
